TPU v7x, 32 devices: a whole 2x2x4 slice. The times are simulated.
32 devices in a mesh: row: 8 (over y, x, core), col: 4 (over z).
Axes of the slice: x: 2, y: 2, z: 4, core: 2. Of those that a mesh axis runs over, the one named last changes fastest.
Arguments:
- pair_rep: bfloat16 [384, 384, 256], P('row', 'col'), may hold values from -6 to 6
- single_rep: bfloat16 [384, 768], replicated, may hold values from -6 to 6
- length: int32 [1], replicated, may hold values from 192 to 384
- pair_gain: float32 [256], replicated, may hold values from 0.25 to 1.75
- pair_proj: bfloat16 [4, 256, 256], replicated, may hold values from -0.375 to 0.375
- bias_weight: bfloat16 [256, 8], replicated, may hold values from -12 to 12
- pair_out_weight: bfloat16 [256, 256], replicated, may hold values from -1 to 1
- single_gain: float32 [768], replicated, may hold values from 0.25 to 1.75
- single_proj: bfloat16 [4, 768, 768], P(None, None, 'col'), may hold values from -0.21875 to 0.21875
- bias_norm_gain: float32 [256], replicated, may hold values from 0.25 to 1.75
- single_bias_weight: bfloat16 [256, 16], replicated, may hold values from -12 to 12
- single_out_weight: bfloat16 [768, 768], P('col'), may hold values from -0.625 to 0.625
Outputs:
- pair_out: bfloat16 [384, 384, 256], P('row', 'col')
- single_out: bfloat16 [384, 768], P('row', 'col')
Inputs may be any that keep to these rules, and one draw needn't show every extreme that they name: Positions from length[0] on are padding and never serve as keys.
All inputs are finite; a program needn't handle non-finite values.
Results may differ from a plain program's by a relative error of at most 0.019.
Values may be sent and summed in bfloat16 or wider, within the bound.
A program may use at most 128 MiB of HBM per device.

v0:
```python
import math

import jax
import jax.numpy as jnp
from jax import lax
from jax.sharding import PartitionSpec as P

PAIR_HEADS = 8
PAIR_HEAD_DIM = 32
SINGLE_HEAD_DIM = 48


masked_value = -1e30


def normalize(values, scales):
    floated = values.astype(jnp.float32)
    center = jnp.mean(floated, axis=-1, keepdims=True)
    spread = jnp.mean(jnp.square(floated - center), axis=-1, keepdims=True)
    return ((floated - center) * lax.rsqrt(spread + 1e-05) * scales).astype(jnp.bfloat16)


def project(inputs, matrix):
    return jnp.dot(inputs, matrix, preferred_element_type=jnp.float32).astype(jnp.bfloat16)


def per_device(
    pair_rep,
    single_rep,
    length,
    pair_gain,
    pair_proj,
    bias_weight,
    pair_out_weight,
    single_gain,
    single_proj,
    bias_norm_gain,
    single_bias_weight,
    single_out_weight,
):
    rows_here, cols_here, channels = pair_rep.shape
    tokens = rows_here * lax.axis_size("row")
    valid_length = length[0]
    pair_scale = 1.0 / math.sqrt(PAIR_HEAD_DIM)
    normed = normalize(pair_rep, pair_gain)
    local_bias = jnp.einsum(
        "rcd,dh->hrc", normed, bias_weight, preferred_element_type=jnp.float32
    ).astype(jnp.bfloat16)
    row_band = lax.all_gather(local_bias, "col", axis=2, tiled=True)
    bias_square = lax.all_gather(row_band, "row", axis=1, tiled=True)
    row_slab = lax.all_to_all(pair_rep, "col", split_axis=0, concat_axis=1, tiled=True)
    slab_rows = row_slab.shape[0]
    slab_normed = normalize(row_slab, pair_gain)
    heads_shape = (slab_rows, tokens, PAIR_HEADS, PAIR_HEAD_DIM)
    slab_query = project(slab_normed, pair_proj[0]).reshape(heads_shape)
    slab_key = project(slab_normed, pair_proj[1]).reshape(heads_shape)
    slab_value = project(slab_normed, pair_proj[2]).reshape(heads_shape)
    slab_gate = jax.nn.sigmoid(
        jnp.dot(slab_normed, pair_proj[3], preferred_element_type=jnp.float32)
    )
    key_usable = jnp.arange(tokens, dtype=jnp.int32) < valid_length

    def whole_row(inputs):
        query_row, key_row, value_row, gate_row, rep_row = inputs
        scores = jnp.einsum("jhd,khd->hjk", query_row, key_row, preferred_element_type=jnp.float32)
        scores = scores * pair_scale + bias_square.astype(jnp.float32)
        scores = jnp.where(key_usable, scores, masked_value)
        row_max = jnp.max(scores, axis=-1, keepdims=True)
        exponent = jnp.exp(scores - row_max)
        weights = (exponent / jnp.sum(exponent, axis=-1, keepdims=True)).astype(jnp.bfloat16)
        attended_row = jnp.einsum(
            "hjk,khd->jhd", weights, value_row, preferred_element_type=jnp.float32
        ).reshape(tokens, channels)
        hidden_row = (gate_row * attended_row).astype(jnp.bfloat16)
        return (
            rep_row.astype(jnp.float32)
            + jnp.dot(hidden_row, pair_out_weight, preferred_element_type=jnp.float32)
        ).astype(jnp.bfloat16)

    updated_slab = lax.map(whole_row, (slab_query, slab_key, slab_value, slab_gate, row_slab))
    pair_out = lax.all_to_all(updated_slab, "col", split_axis=1, concat_axis=0, tiled=True)
    bias_normed = normalize(pair_out, bias_norm_gain)
    pair_bias = jnp.einsum(
        "rcd,dh->hrc", bias_normed, single_bias_weight, preferred_element_type=jnp.float32
    ).astype(jnp.bfloat16)
    head_bias = lax.all_to_all(pair_bias, "col", split_axis=0, concat_axis=2, tiled=True)
    single_normed = normalize(single_rep, single_gain)
    row_start = lax.axis_index("row") * rows_here
    mine = lax.dynamic_slice_in_dim(single_normed, row_start, rows_here, 0)
    local_width = single_proj.shape[2]
    heads_here = local_width // SINGLE_HEAD_DIM
    s_query = project(mine, single_proj[0]).reshape(rows_here, heads_here, SINGLE_HEAD_DIM)
    s_key = project(single_normed, single_proj[1]).reshape(tokens, heads_here, SINGLE_HEAD_DIM)
    s_value = project(single_normed, single_proj[2]).reshape(tokens, heads_here, SINGLE_HEAD_DIM)
    s_gate = jax.nn.sigmoid(jnp.dot(mine, single_proj[3], preferred_element_type=jnp.float32))
    scores = jnp.einsum(
        "ihd,jhd->hij", s_query, s_key, preferred_element_type=jnp.float32
    ) / math.sqrt(SINGLE_HEAD_DIM)
    scores = scores + head_bias.astype(jnp.float32)
    token_usable = jnp.arange(tokens, dtype=jnp.int32) < valid_length
    scores = jnp.where(token_usable, scores, masked_value)
    row_max = jnp.max(scores, axis=-1, keepdims=True)
    exponent = jnp.exp(scores - row_max)
    weights = (exponent / jnp.sum(exponent, axis=-1, keepdims=True)).astype(jnp.bfloat16)
    blended = jnp.einsum(
        "hij,jhd->ihd", weights, s_value, preferred_element_type=jnp.float32
    ).reshape(rows_here, local_width)
    s_hidden = (s_gate * blended).astype(jnp.bfloat16)
    partial_value = jnp.dot(s_hidden, single_out_weight, preferred_element_type=jnp.float32)
    reduced = lax.psum_scatter(
        partial_value.astype(jnp.bfloat16), "col", scatter_dimension=1, tiled=True
    ).astype(jnp.float32)
    col_start = lax.axis_index("col") * local_width
    residual = lax.dynamic_slice(single_rep, (row_start, col_start), (rows_here, local_width))
    single_out = (residual.astype(jnp.float32) + reduced).astype(jnp.bfloat16)
    return (pair_out, single_out)


def solution(mesh):
    in_specs = (
        P("row", "col", None),
        P(),
        P(),
        P(),
        P(),
        P(),
        P(),
        P(),
        P(None, None, "col"),
        P(),
        P(),
        P("col", None),
    )
    out_specs = (P("row", "col", None), P("row", "col"))
    return jax.shard_map(
        per_device, mesh=mesh, in_specs=in_specs, out_specs=out_specs, check_vma=False
    )
```

profile of v0, /device:TPU:0, one launch (start us, length us, event | category | flops | bytes accessed | tf_op | source)
XLA Modules:
  0.0 392.2 jit_solution(9332330471362838107)
XLA Ops:
  7.2 6.5 %all-to-all-start = ((bf16[48,96,256]{2,1,0:T(8,128)(2,1)}), bf16[48,96,256]{2,1,0:T(8,128)(2,1)S(1)}, u32[]{:S(2)}, u32[]{:S(2)}) async-start(bf16[48,96,256]{2,1,0:T(8,128)(2,1)} %param.14), calls=%async_computation | async-start | bytes 4718592 | tf_op jit(solution)/shard_map/all_to_all | solution.py:51
  13.7 2.7 convert_reduce_fusion.1
  18.2 2.0 fusion.82
  21.0 60.0 %all_gather.6 = bf16[8,48,384]{1,0,2:T(8,128)(2,1)S(1)} all-gather(bf16[8,48,96]{1,0,2:T(8,128)(2,1)} %copy.72), channel_id=1, replica_groups=mesh['row'=8,'col'=4] {'col'}, dimensions={2}, use_global_device_ids=true | all-gather | bytes 368640 | tf_op jit(solution)/shard_map/all_gather | solution.py:49
  88.2 2.2 convolution_convert_fusion.1
  90.5 2.3 convolution_convert_fusion
  92.8 2.3 convolution_convert_fusion.2
  95.1 3.5 add_divide_fusion
  98.7 13.4 %all-gather.2.cloned.1.call-done = bf16[8,384,384]{2,0,1:T(8,128)(2,1)} async-done(((bf16[8,48,384]{2,0,1:T(8,128)(2,1)}), bf16[8,384,384]{2,0,1:T(8,128)(2,1)}) %all-gather.2.cloned.1.call-update) | async-done | bytes 2359312 | tf_op jit(solution)/shard_map/all_gather | solution.py:50
  112.1 4.5 %copy.75 = bf16[8,384,384]{1,2,0:T(8,128)(2,1)} copy(bf16[8,384,384]{2,0,1:T(8,128)(2,1)} %all-gather.2.cloned.1.call-done) | data formatting | bytes 4718592
  116.5 142.8 %while.11 = (s32[]{:T(128)}, bf16[12,384,256]{2,1,0:T(8,128)(2,1)}, bf16[12,384,256]{2,1,0:T(8,128)(2,1)}, f32[12,384,256]{2,1,0:T(8,128)}, bf16[12,384,8,32]{1,...) while((s32[]{:T(128)}, bf16[12,384,256]{2,1,0:T(8,128)(2,1)}, ...), condition=%wide.region_7.8_spmd.clone, body=%wide.region_4.7_spmd.clone.sunk | while | flops 292655232 | bytes 9400565 | solution.py:80
  117.2 3.9 fusion.158
  121.1 4.2 %fusion.159 = f32[8,32,384]{2,1,0:T(8,128)S(1)} fusion(f32[8,384]{1,0:T(8,128)S(1)} %fusion.158, bf16[12,384,8,32]{1,3,2,0:T(8,128)(2,1)} %get-tuple-element.235, s32[]{:T(128)} %get-tuple-element.220, bf16[8,384,384]{1,2,0:T(8,128)(2,1)} %get-tuple-element.238, pred[384]{0:T(512)(128)(4,1)S(1)} %iota_compare_fusion.3, ...), kind=kOutput, calls=%fused_computation.9.clone.1 | convolution fusion | flops 159255936 | bytes 3356544 | tf_op jit(solution)/shard_map/while/body/eval_jaxpr/hjk,khd->jhd/dot_general | solution.py:71
  129.1 3.9 fusion.158
  133.0 4.2 %fusion.159 = f32[8,32,384]{2,1,0:T(8,128)S(1)} fusion(f32[8,384]{1,0:T(8,128)S(1)} %fusion.158, bf16[12,384,8,32]{1,3,2,0:T(8,128)(2,1)} %get-tuple-element.235, s32[]{:T(128)} %get-tuple-element.220, bf16[8,384,384]{1,2,0:T(8,128)(2,1)} %get-tuple-element.238, pred[384]{0:T(512)(128)(4,1)S(1)} %iota_compare_fusion.3, ...), kind=kOutput, calls=%fused_computation.9.clone.1 | convolution fusion | flops 159255936 | bytes 3356544 | tf_op jit(solution)/shard_map/while/body/eval_jaxpr/hjk,khd->jhd/dot_general | solution.py:71
  141.0 3.9 fusion.158
  144.9 4.2 %fusion.159 = f32[8,32,384]{2,1,0:T(8,128)S(1)} fusion(f32[8,384]{1,0:T(8,128)S(1)} %fusion.158, bf16[12,384,8,32]{1,3,2,0:T(8,128)(2,1)} %get-tuple-element.235, s32[]{:T(128)} %get-tuple-element.220, bf16[8,384,384]{1,2,0:T(8,128)(2,1)} %get-tuple-element.238, pred[384]{0:T(512)(128)(4,1)S(1)} %iota_compare_fusion.3, ...), kind=kOutput, calls=%fused_computation.9.clone.1 | convolution fusion | flops 159255936 | bytes 3356544 | tf_op jit(solution)/shard_map/while/body/eval_jaxpr/hjk,khd->jhd/dot_general | solution.py:71
  150.4 1.9 fusion.161
  152.9 3.9 fusion.158
  156.8 4.2 %fusion.159 = f32[8,32,384]{2,1,0:T(8,128)S(1)} fusion(f32[8,384]{1,0:T(8,128)S(1)} %fusion.158, bf16[12,384,8,32]{1,3,2,0:T(8,128)(2,1)} %get-tuple-element.235, s32[]{:T(128)} %get-tuple-element.220, bf16[8,384,384]{1,2,0:T(8,128)(2,1)} %get-tuple-element.238, pred[384]{0:T(512)(128)(4,1)S(1)} %iota_compare_fusion.3, ...), kind=kOutput, calls=%fused_computation.9.clone.1 | convolution fusion | flops 159255936 | bytes 3356544 | tf_op jit(solution)/shard_map/while/body/eval_jaxpr/hjk,khd->jhd/dot_general | solution.py:71
  164.8 3.9 fusion.158
  168.7 4.2 %fusion.159 = f32[8,32,384]{2,1,0:T(8,128)S(1)} fusion(f32[8,384]{1,0:T(8,128)S(1)} %fusion.158, bf16[12,384,8,32]{1,3,2,0:T(8,128)(2,1)} %get-tuple-element.235, s32[]{:T(128)} %get-tuple-element.220, bf16[8,384,384]{1,2,0:T(8,128)(2,1)} %get-tuple-element.238, pred[384]{0:T(512)(128)(4,1)S(1)} %iota_compare_fusion.3, ...), kind=kOutput, calls=%fused_computation.9.clone.1 | convolution fusion | flops 159255936 | bytes 3356544 | tf_op jit(solution)/shard_map/while/body/eval_jaxpr/hjk,khd->jhd/dot_general | solution.py:71
  176.7 3.9 fusion.158
  180.6 4.2 %fusion.159 = f32[8,32,384]{2,1,0:T(8,128)S(1)} fusion(f32[8,384]{1,0:T(8,128)S(1)} %fusion.158, bf16[12,384,8,32]{1,3,2,0:T(8,128)(2,1)} %get-tuple-element.235, s32[]{:T(128)} %get-tuple-element.220, bf16[8,384,384]{1,2,0:T(8,128)(2,1)} %get-tuple-element.238, pred[384]{0:T(512)(128)(4,1)S(1)} %iota_compare_fusion.3, ...), kind=kOutput, calls=%fused_computation.9.clone.1 | convolution fusion | flops 159255936 | bytes 3356544 | tf_op jit(solution)/shard_map/while/body/eval_jaxpr/hjk,khd->jhd/dot_general | solution.py:71
  188.6 3.9 fusion.158
  192.5 4.2 %fusion.159 = f32[8,32,384]{2,1,0:T(8,128)S(1)} fusion(f32[8,384]{1,0:T(8,128)S(1)} %fusion.158, bf16[12,384,8,32]{1,3,2,0:T(8,128)(2,1)} %get-tuple-element.235, s32[]{:T(128)} %get-tuple-element.220, bf16[8,384,384]{1,2,0:T(8,128)(2,1)} %get-tuple-element.238, pred[384]{0:T(512)(128)(4,1)S(1)} %iota_compare_fusion.3, ...), kind=kOutput, calls=%fused_computation.9.clone.1 | convolution fusion | flops 159255936 | bytes 3356544 | tf_op jit(solution)/shard_map/while/body/eval_jaxpr/hjk,khd->jhd/dot_general | solution.py:71
  200.5 3.9 fusion.158
  204.4 4.2 %fusion.159 = f32[8,32,384]{2,1,0:T(8,128)S(1)} fusion(f32[8,384]{1,0:T(8,128)S(1)} %fusion.158, bf16[12,384,8,32]{1,3,2,0:T(8,128)(2,1)} %get-tuple-element.235, s32[]{:T(128)} %get-tuple-element.220, bf16[8,384,384]{1,2,0:T(8,128)(2,1)} %get-tuple-element.238, pred[384]{0:T(512)(128)(4,1)S(1)} %iota_compare_fusion.3, ...), kind=kOutput, calls=%fused_computation.9.clone.1 | convolution fusion | flops 159255936 | bytes 3356544 | tf_op jit(solution)/shard_map/while/body/eval_jaxpr/hjk,khd->jhd/dot_general | solution.py:71
  212.4 3.9 fusion.158
  216.3 4.2 %fusion.159 = f32[8,32,384]{2,1,0:T(8,128)S(1)} fusion(f32[8,384]{1,0:T(8,128)S(1)} %fusion.158, bf16[12,384,8,32]{1,3,2,0:T(8,128)(2,1)} %get-tuple-element.235, s32[]{:T(128)} %get-tuple-element.220, bf16[8,384,384]{1,2,0:T(8,128)(2,1)} %get-tuple-element.238, pred[384]{0:T(512)(128)(4,1)S(1)} %iota_compare_fusion.3, ...), kind=kOutput, calls=%fused_computation.9.clone.1 | convolution fusion | flops 159255936 | bytes 3356544 | tf_op jit(solution)/shard_map/while/body/eval_jaxpr/hjk,khd->jhd/dot_general | solution.py:71
  221.8 1.9 fusion.161
  224.3 3.9 fusion.158
  228.2 4.2 %fusion.159 = f32[8,32,384]{2,1,0:T(8,128)S(1)} fusion(f32[8,384]{1,0:T(8,128)S(1)} %fusion.158, bf16[12,384,8,32]{1,3,2,0:T(8,128)(2,1)} %get-tuple-element.235, s32[]{:T(128)} %get-tuple-element.220, bf16[8,384,384]{1,2,0:T(8,128)(2,1)} %get-tuple-element.238, pred[384]{0:T(512)(128)(4,1)S(1)} %iota_compare_fusion.3, ...), kind=kOutput, calls=%fused_computation.9.clone.1 | convolution fusion | flops 159255936 | bytes 3356544 | tf_op jit(solution)/shard_map/while/body/eval_jaxpr/hjk,khd->jhd/dot_general | solution.py:71
  236.2 3.9 fusion.158
  240.1 4.2 %fusion.159 = f32[8,32,384]{2,1,0:T(8,128)S(1)} fusion(f32[8,384]{1,0:T(8,128)S(1)} %fusion.158, bf16[12,384,8,32]{1,3,2,0:T(8,128)(2,1)} %get-tuple-element.235, s32[]{:T(128)} %get-tuple-element.220, bf16[8,384,384]{1,2,0:T(8,128)(2,1)} %get-tuple-element.238, pred[384]{0:T(512)(128)(4,1)S(1)} %iota_compare_fusion.3, ...), kind=kOutput, calls=%fused_computation.9.clone.1 | convolution fusion | flops 159255936 | bytes 3356544 | tf_op jit(solution)/shard_map/while/body/eval_jaxpr/hjk,khd->jhd/dot_general | solution.py:71
  245.6 1.9 fusion.161
  248.1 3.9 fusion.158
  252.0 4.2 %fusion.159 = f32[8,32,384]{2,1,0:T(8,128)S(1)} fusion(f32[8,384]{1,0:T(8,128)S(1)} %fusion.158, bf16[12,384,8,32]{1,3,2,0:T(8,128)(2,1)} %get-tuple-element.235, s32[]{:T(128)} %get-tuple-element.220, bf16[8,384,384]{1,2,0:T(8,128)(2,1)} %get-tuple-element.238, pred[384]{0:T(512)(128)(4,1)S(1)} %iota_compare_fusion.3, ...), kind=kOutput, calls=%fused_computation.9.clone.1 | convolution fusion | flops 159255936 | bytes 3356544 | tf_op jit(solution)/shard_map/while/body/eval_jaxpr/hjk,khd->jhd/dot_general | solution.py:71
  259.4 4.7 %copy.76 = bf16[12,384,256]{2,0,1:T(8,128)(2,1)} copy(bf16[12,384,256]{2,1,0:T(8,128)(2,1)} %get-tuple-element.54) | data formatting | bytes 4718592 | tf_op jit(solution)/shard_map/while | solution.py:80
  264.1 4.7 %all-to-all-start.1 = ((bf16[12,384,256]{2,0,1:T(8,128)(2,1)}), bf16[12,384,256]{2,0,1:T(8,128)(2,1)S(1)}, u32[]{:S(2)}, u32[]{:S(2)}) async-start(bf16[12,384,256]{2,0,1:T(8,128)(2,1)} %copy.76), calls=%async_computation.1 | async-start | bytes 6291456 | tf_op jit(solution)/shard_map/all_to_all | solution.py:81
  275.5 2.2 convolution_convert_fusion.3
  277.7 62.2 %all-to-all-done.1 = bf16[12,384,256]{2,0,1:T(8,128)(2,1)S(1)} async-done(((bf16[12,384,256]{2,0,1:T(8,128)(2,1)}), bf16[12,384,256]{2,0,1:T(8,128)(2,1)S(1)}, u32[]{:S(2)}, u32[]{:S(2)}) %all-to-all-start.1) | async-done | bytes 2359328 | tf_op jit(solution)/shard_map/all_to_all | solution.py:81
  340.8 2.3 copy.77
  343.8 2.5 fusion.54
  348.5 3.0 fusion.78
  352.2 3.4 all-to-all-start.2
  356.0 6.8 %all-to-all-done.2 = bf16[16,48,96]{2,1,0:T(8,128)(2,1)S(1)} async-done(((bf16[16,48,96]{2,1,0:T(8,128)(2,1)}), bf16[16,48,96]{2,1,0:T(8,128)(2,1)S(1)}, u32[]{:S(2)}, u32[]{:S(2)}) %all-to-all-start.2) | async-done | bytes 147488 | tf_op jit(solution)/shard_map/all_to_all | solution.py:86
  365.4 17.6 %reduce-scatter.4.cloned.1.call-done = bf16[192,48]{1,0:T(8,128)(2,1)} async-done(((bf16[768,48]{1,0:T(8,128)(2,1)}), bf16[192,48]{1,0:T(8,128)(2,1)}) %reduce-scatter.4.cloned.1.call-update) | async-done | bytes 18448
  (129 shorter events, 64.9 us)
Async XLA Ops:
  7.2 357.0 %copy-start = (bf16[192,768]{1,0:T(8,128)(2,1)S(1)}, bf16[192,768]{1,0:T(8,128)(2,1)}, u32[]{:S(2)}) copy-start(bf16[192,768]{1,0:T(8,128)(2,1)} %param.25) | copy-start | bytes 884740
  7.2 75.1 %all-to-all-start = ((bf16[48,96,256]{2,1,0:T(8,128)(2,1)}), bf16[48,96,256]{2,1,0:T(8,128)(2,1)S(1)}, u32[]{:S(2)}, u32[]{:S(2)}) async-start(bf16[48,96,256]{2,1,0:T(8,128)(2,1)} %param.14), calls=%async_computation | async-start | bytes 4718592 | tf_op jit(solution)/shard_map/all_to_all | solution.py:51
  13.7 4.5 %copy-start.9 = (f32[256]{0:T(256)S(1)}, f32[256]{0:T(256)}, u32[]{:S(2)}) copy-start(f32[256]{0:T(256)} %param.17) | copy-start | bytes 3076
  13.7 4.5 %copy-start.12 = (bf16[256,8]{0,1:T(8,128)(2,1)S(1)}, bf16[256,8]{0,1:T(8,128)(2,1)}, u32[]{:S(2)}) copy-start(bf16[256,8]{0,1:T(8,128)(2,1)} %param.19) | copy-start | bytes 12292
  13.7 98.4 %all-gather.2.cloned.1.call-start = ((), (), s32[]{:S(2)}) async-start(), calls=%async_computation.4 | async-start | bytes 2654208 | tf_op jit(solution)/shard_map/all_gather | solution.py:50
  13.7 2.7 copy-start.1
  86.7 1.5 copy-start.6
  98.7 17.9 %copy-start.2 = (bf16[256,256]{1,0:T(8,128)(2,1)S(1)}, bf16[256,256]{1,0:T(8,128)(2,1)}, u32[]{:S(2)}) copy-start(bf16[256,256]{1,0:T(8,128)(2,1)} %param.20) | copy-start | bytes 393220
  264.1 8.0 %copy-start.8 = (f32[768]{0:T(1024)S(1)}, f32[768]{0:T(1024)}, u32[]{:S(2)}) copy-start(f32[768]{0:T(1024)} %param.21) | copy-start | bytes 9220
  264.1 75.8 %all-to-all-start.1 = ((bf16[12,384,256]{2,0,1:T(8,128)(2,1)}), bf16[12,384,256]{2,0,1:T(8,128)(2,1)S(1)}, u32[]{:S(2)}, u32[]{:S(2)}) async-start(bf16[12,384,256]{2,0,1:T(8,128)(2,1)} %copy.76), calls=%async_computation.1 | async-start | bytes 6291456 | tf_op jit(solution)/shard_map/all_to_all | solution.py:81
  273.4 0.8 copy-start.4
  343.1 5.4 %copy-start.11 = (bf16[256,16]{0,1:T(8,128)(2,1)S(1)}, bf16[256,16]{0,1:T(8,128)(2,1)}, u32[]{:S(2)}) copy-start(bf16[256,16]{0,1:T(8,128)(2,1)} %param.24) | copy-start | bytes 24580
  343.1 5.4 %copy-start.13 = (f32[256]{0:T(256)S(1)}, f32[256]{0:T(256)}, u32[]{:S(2)}) copy-start(f32[256]{0:T(256)} %param.23) | copy-start | bytes 3076
  343.1 0.7 copy-start.3
  348.5 7.2 %copy-start.5 = (bf16[384,768]{1,0:T(8,128)(2,1)S(1)}, bf16[384,768]{1,0:T(8,128)(2,1)}, u32[]{:S(2)}) copy-start(bf16[384,768]{1,0:T(8,128)(2,1)} %copy-done.4) | copy-start | bytes 1769476
  348.5 7.2 %copy-start.10 = (bf16[4,768,192]{1,2,0:T(8,128)(2,1)S(1)}, bf16[4,768,192]{1,2,0:T(8,128)(2,1)}, u32[]{:S(2)}) copy-start(bf16[4,768,192]{1,2,0:T(8,128)(2,1)} %param.22) | copy-start | bytes 3538948
  351.5 11.7 %copy-start.7 = (bf16[384,192]{0,1:T(8,128)(2,1)S(1)}, bf16[384,192]{0,1:T(8,128)(2,1)}, u32[]{:S(2)}) copy-start(bf16[384,192]{0,1:T(8,128)(2,1)} %convolution_convert_fusion.3) | copy-start | bytes 442372
  352.2 10.6 %all-to-all-start.2 = ((bf16[16,48,96]{2,1,0:T(8,128)(2,1)}), bf16[16,48,96]{2,1,0:T(8,128)(2,1)S(1)}, u32[]{:S(2)}, u32[]{:S(2)}) async-start(bf16[16,48,96]{2,1,0:T(8,128)(2,1)} %copy.84), calls=%async_computation.2 | async-start | bytes 393216 | tf_op jit(solution)/shard_map/all_to_all | solution.py:86
  355.6 27.4 %reduce-scatter.4.cloned.1.call-start = ((), (), s32[]{:S(2)}) async-start(), calls=%async_computation.5 | async-start | bytes 245760
Sparse Core Ops, SparseCore 0:
  82.4 29.6 all-gather.1
  365.5 17.4 reduce-scatter.3
where the time goes:
time: 395 us; the launch traced here: 392 us
  matrix products  140 us (35%)
  waiting for transfers between devices  100 us (25%)
  blocking collectives  60 us (15%)
  local copies, waits for them, and re-layouts  35.2 us (9%)
  other arithmetic  26.9 us (7%)
  between operations  15 us (4%)
  starting transfers between devices  14.7 us (4%)
    all_to_all x1, waiting for transfers between devices, per_device(): lax.all_to_all(updated_slab, 'col', split_axis=1, concat_axis=0, tiled=True)  62.2 us
    all_gather x1, blocking collectives, per_device(): row_band = lax.all_gather(local_bias, 'col', axis=2, tiled=True)  60 us
    dot_general x12, matrix products, whole_row(): jnp.einsum('hjk,khd->jhd', weights, value_row, preferred_element_type=jnp...  50.6 us
    sub x12, matrix products, whole_row(): exponent = jnp.exp(scores - row_max)  46.9 us
    dot_general x12, matrix products, whole_row(): jnp.dot(hidden_row, pair_out_weight, preferred_element_type=jnp.float32)  22.5 us
    unnamed x3, waiting for transfers between devices  17.7 us
    dynamic_slice x24, local copies, waits for them, and re-layouts, per_device(): lax.map(whole_row, (slab_query, slab_key, slab_value, slab_gate, row_slab))  14.3 us
    all_gather x1, waiting for transfers between devices, per_device(): bias_square = lax.all_gather(row_band, 'row', axis=1, tiled=True)  13.4 us
  transfers between devices with their start and end apart: 5, of which 4 were waited for; matrix products, arithmetic and copies ran while one was open for 8% of the time, Pallas kernels for 0%

commit v1 on v0

--- a/solution.py
+++ b/solution.py
@@ -3,14 +3,17 @@
 import jax
 import jax.numpy as jnp
 from jax import lax
+from jax.experimental import pallas as pl
+from jax.experimental.pallas import tpu as pltpu
 from jax.sharding import PartitionSpec as P
 
 PAIR_HEADS = 8
 PAIR_HEAD_DIM = 32
 SINGLE_HEAD_DIM = 48
-
+LOG2E = math.log2(math.e)
 
 masked_value = -1e30
+NT = (((1,), (1,)), ((), ()))
 
 
 def normalize(values, scales):
@@ -22,6 +25,102 @@
 
 def project(inputs, matrix):
     return jnp.dot(inputs, matrix, preferred_element_type=jnp.float32).astype(jnp.bfloat16)
+
+
+def row_update(rep, gain, proj_ref, out_weight, bias_of):
+    channels = rep.shape[1]
+    half = channels // 2
+    heads_per_half = PAIR_HEADS // 2
+    normed = normalize(rep, gain)
+    f32 = jnp.float32
+    query = jnp.dot(normed, proj_ref[0], preferred_element_type=f32)
+    query = (query * (LOG2E / math.sqrt(PAIR_HEAD_DIM))).astype(jnp.bfloat16)
+    key = project(normed, proj_ref[1])
+    value = project(normed, proj_ref[2])
+    gate = jax.nn.sigmoid(jnp.dot(normed, proj_ref[3], preferred_element_type=f32))
+    head_of_lane = lax.broadcasted_iota(jnp.int32, (1, half), 1) // PAIR_HEAD_DIM
+    halves = []
+    for side in range(2):
+        span = slice(side * half, (side + 1) * half)
+        q_half, k_half, v_half = query[:, span], key[:, span], value[:, span]
+        top = bottom = None
+        for sub in range(heads_per_half):
+            head = side * heads_per_half + sub
+            mine = head_of_lane == sub
+            q_head = jnp.where(mine, q_half, jnp.zeros_like(q_half))
+            scores = lax.dot_general(q_head, k_half, NT, preferred_element_type=f32)
+            scores = scores + bias_of(head)
+            peak = jnp.max(scores, axis=-1, keepdims=True)
+            exponent = jnp.exp2(scores - peak).astype(jnp.bfloat16)
+            v_ext = jnp.concatenate([v_half, jnp.ones_like(v_half)], axis=1)
+            both = jnp.dot(exponent, v_ext, preferred_element_type=f32)
+            num, den = both[:, :half], both[:, half:]
+            top = num if top is None else jnp.where(mine, num, top)
+            bottom = den if bottom is None else jnp.where(mine, den, bottom)
+        halves.append(top / bottom)
+    attended = jnp.concatenate(halves, axis=1)
+    hidden = (gate * attended).astype(jnp.bfloat16)
+    return (
+        rep.astype(f32) + jnp.dot(hidden, out_weight, preferred_element_type=f32)
+    ).astype(jnp.bfloat16)
+
+
+def slab_kernel(
+    length_ref, rep_ref, bias_ref, gain_ref, proj_ref, out_weight_ref, bias_gain_ref, head_weight_ref,
+    new_ref, head_bias_ref, bias_held,
+):
+    bands, heads, band_rows, tokens = bias_ref.shape
+
+    @pl.when(pl.program_id(0) == 0)
+    def _():
+        usable = lax.broadcasted_iota(jnp.int32, (1, 1, tokens), 2) < length_ref[0]
+        for band in range(bands):
+            piece = bias_ref[band].astype(jnp.float32) * LOG2E
+            bias_held[:, band * band_rows : (band + 1) * band_rows, :] = jnp.where(
+                usable, piece, masked_value
+            )
+
+    updated = row_update(
+        rep_ref[0], gain_ref[...], proj_ref, out_weight_ref[...], lambda head: bias_held[head]
+    )
+    new_ref[0] = updated
+    again = normalize(updated, bias_gain_ref[...])
+    head_bias_ref[0] = lax.dot_general(
+        head_weight_ref[...], again, NT, preferred_element_type=jnp.float32
+    ).astype(jnp.bfloat16)
+
+
+def slab_attention(length, slab, bias, gain, proj, out_weight, bias_gain, head_weight_t):
+    rows, tokens, channels = slab.shape
+    single_heads = head_weight_t.shape[0]
+    whole = lambda shape: pl.BlockSpec(
+        shape, lambda i: (0,) * len(shape), pipeline_mode=pl.Buffered(1)
+    )
+    return pl.pallas_call(
+        slab_kernel,
+        grid=(rows,),
+        in_specs=[
+            pl.BlockSpec(memory_space=pltpu.SMEM),
+            pl.BlockSpec((1, tokens, channels), lambda i: (i, 0, 0)),
+            whole(bias.shape),
+            whole((1, channels)),
+            whole(proj.shape),
+            whole(out_weight.shape),
+            whole((1, channels)),
+            whole(head_weight_t.shape),
+        ],
+        out_specs=[
+            pl.BlockSpec((1, tokens, channels), lambda i: (i, 0, 0)),
+            pl.BlockSpec((1, single_heads, tokens), lambda i: (i, 0, 0)),
+        ],
+        out_shape=[
+            jax.ShapeDtypeStruct(slab.shape, jnp.bfloat16),
+            jax.ShapeDtypeStruct((rows, single_heads, tokens), jnp.bfloat16),
+        ],
+        scratch_shapes=[pltpu.VMEM((PAIR_HEADS, tokens, tokens), jnp.float32)],
+        compiler_params=pltpu.CompilerParams(vmem_limit_bytes=60 * 2**20),
+        name="slab_attention",
+    )(length, slab, bias, gain, proj, out_weight, bias_gain, head_weight_t)
 
 
 def per_device(
@@ -41,49 +140,26 @@
     rows_here, cols_here, channels = pair_rep.shape
     tokens = rows_here * lax.axis_size("row")
     valid_length = length[0]
-    pair_scale = 1.0 / math.sqrt(PAIR_HEAD_DIM)
     normed = normalize(pair_rep, pair_gain)
     local_bias = jnp.einsum(
         "rcd,dh->hrc", normed, bias_weight, preferred_element_type=jnp.float32
     ).astype(jnp.bfloat16)
     row_band = lax.all_gather(local_bias, "col", axis=2, tiled=True)
-    bias_square = lax.all_gather(row_band, "row", axis=1, tiled=True)
+    bias_bands = lax.all_gather(row_band, "row")
     row_slab = lax.all_to_all(pair_rep, "col", split_axis=0, concat_axis=1, tiled=True)
-    slab_rows = row_slab.shape[0]
-    slab_normed = normalize(row_slab, pair_gain)
-    heads_shape = (slab_rows, tokens, PAIR_HEADS, PAIR_HEAD_DIM)
-    slab_query = project(slab_normed, pair_proj[0]).reshape(heads_shape)
-    slab_key = project(slab_normed, pair_proj[1]).reshape(heads_shape)
-    slab_value = project(slab_normed, pair_proj[2]).reshape(heads_shape)
-    slab_gate = jax.nn.sigmoid(
-        jnp.dot(slab_normed, pair_proj[3], preferred_element_type=jnp.float32)
-    )
-    key_usable = jnp.arange(tokens, dtype=jnp.int32) < valid_length
-
-    def whole_row(inputs):
-        query_row, key_row, value_row, gate_row, rep_row = inputs
-        scores = jnp.einsum("jhd,khd->hjk", query_row, key_row, preferred_element_type=jnp.float32)
-        scores = scores * pair_scale + bias_square.astype(jnp.float32)
-        scores = jnp.where(key_usable, scores, masked_value)
-        row_max = jnp.max(scores, axis=-1, keepdims=True)
-        exponent = jnp.exp(scores - row_max)
-        weights = (exponent / jnp.sum(exponent, axis=-1, keepdims=True)).astype(jnp.bfloat16)
-        attended_row = jnp.einsum(
-            "hjk,khd->jhd", weights, value_row, preferred_element_type=jnp.float32
-        ).reshape(tokens, channels)
-        hidden_row = (gate_row * attended_row).astype(jnp.bfloat16)
-        return (
-            rep_row.astype(jnp.float32)
-            + jnp.dot(hidden_row, pair_out_weight, preferred_element_type=jnp.float32)
-        ).astype(jnp.bfloat16)
-
-    updated_slab = lax.map(whole_row, (slab_query, slab_key, slab_value, slab_gate, row_slab))
+    updated_slab, slab_head_bias = slab_attention(
+        length,
+        row_slab,
+        bias_bands,
+        pair_gain[None],
+        pair_proj,
+        pair_out_weight,
+        bias_norm_gain[None],
+        single_bias_weight.T,
+    )
     pair_out = lax.all_to_all(updated_slab, "col", split_axis=1, concat_axis=0, tiled=True)
-    bias_normed = normalize(pair_out, bias_norm_gain)
-    pair_bias = jnp.einsum(
-        "rcd,dh->hrc", bias_normed, single_bias_weight, preferred_element_type=jnp.float32
-    ).astype(jnp.bfloat16)
-    head_bias = lax.all_to_all(pair_bias, "col", split_axis=0, concat_axis=2, tiled=True)
+    head_bias = lax.all_to_all(slab_head_bias, "col", split_axis=1, concat_axis=0, tiled=True)
+    head_bias = jnp.transpose(head_bias, (1, 0, 2))
     single_normed = normalize(single_rep, single_gain)
     row_start = lax.axis_index("row") * rows_here
     mine = lax.dynamic_slice_in_dim(single_normed, row_start, rows_here, 0)

time: 395 us -> 247 us (0.63)
  matrix products: 140 us -> 10.8 us
  Pallas kernels: 0 us -> 45.4 us
  blocking collectives: 60 us -> 21.7 us
  other arithmetic: 26.9 us -> 11.1 us
  local copies, waits for them, and re-layouts: 35.2 us -> 25.1 us
  waiting for transfers between devices: 100 us -> 106 us
    dot_general x26 -> x0, matrix products: 79.6 us -> none  [the longest x12 50.6 us: whole_row(): jnp.einsum('hjk,khd->jhd', weights, value_row, preferred_element_type=jnp...]
    all_to_all x1, waiting for transfers between devices: 0.01 us -> 50.8 us  [per_device(): lax.all_to_all(pair_rep, 'col', split_axis=0, concat_axis=1, tiled=True)]
    all_to_all x1, waiting for transfers between devices: 62.2 us -> 13.2 us  [per_device(): lax.all_to_all(updated_slab, 'col', split_axis=1, concat_axis=0, tiled=True)]
    sub x12 -> x0, matrix products: 46.9 us -> none  [whole_row(): exponent = jnp.exp(scores - row_max)]
    pallas_call x0 -> x1, Pallas kernels: none -> 45.4 us  [slab_attention(): pl.pallas_call(slab_kernel, grid=(rows,), in_specs=[pl.BlockSpec(memory_s...]
    all_gather x1, blocking collectives: 60 us -> 21.7 us  [per_device(): row_band = lax.all_gather(local_bias, 'col', axis=2, tiled=True)]
    unnamed x3, waiting for transfers between devices: 17.7 us -> 39.7 us
    dynamic_slice x24 -> x0, local copies, waits for them, and re-layouts: 14.3 us -> none  [per_device(): lax.map(whole_row, (slab_query, slab_key, slab_value, slab_gate, row_slab))]
  transfers between devices with their start and end apart: 5 -> 5, of which waited for: 4 -> 4; matrix products, arithmetic and copies ran while one was open for 8% -> 10% of each run, Pallas kernels for 0% -> 0%
where the time goes in v1:
time: 247 us; the launch traced here: 246 us
  waiting for transfers between devices  106 us (43%)
  Pallas kernels  45.4 us (18%)
  local copies, waits for them, and re-layouts  25.1 us (10%)
  blocking collectives  21.7 us (9%)
  between operations  14.9 us (6%)
  other arithmetic  11.1 us (4%)
  starting transfers between devices  11 us (4%)
  matrix products  10.8 us (4%)
    all_to_all x1, waiting for transfers between devices, per_device(): lax.all_to_all(pair_rep, 'col', split_axis=0, concat_axis=1, tiled=True)  50.8 us
    pallas_call x1, Pallas kernels, slab_attention(): pl.pallas_call(slab_kernel, grid=(rows,), in_specs=[pl.BlockSpec(memory_s...  45.4 us
    unnamed x3, waiting for transfers between devices  39.7 us
    all_gather x1, blocking collectives, per_device(): row_band = lax.all_gather(local_bias, 'col', axis=2, tiled=True)  21.7 us
    all_to_all x1, waiting for transfers between devices, per_device(): lax.all_to_all(updated_slab, 'col', split_axis=1, concat_axis=0, tiled=True)  13.2 us
    all_gather x1, local copies, waits for them, and re-layouts, per_device(): bias_bands = lax.all_gather(row_band, 'row')  8.92 us
    pallas_call x2, local copies, waits for them, and re-layouts, slab_attention(): pl.pallas_call(slab_kernel, grid=(rows,), in_specs=[pl.BlockSpec(memory_s...  6.37 us
  transfers between devices with their start and end apart: 5, of which 4 were waited for; matrix products, arithmetic and copies ran while one was open for 10% of the time, Pallas kernels for 0%

profile of v1, /device:TPU:0, one launch (start us, length us, event | category | flops | bytes accessed | tf_op | source)
XLA Modules:
  0.0 246.1 jit_solution(5074205689633292723)
XLA Ops:
  7.2 0.0 copy-start
  7.2 0.0 copy-start.5
  7.2 0.0 copy-start.6
  7.2 0.0 all-gather.3.cloned.1.call-start
  7.2 2.6 %convert_reduce_fusion = f32[48,96]{1,0:T(8,128)S(1)} fusion(bf16[48,96,256]{2,1,0:T(8,128)(2,1)} %param.12), kind=kLoop, calls=%fused_computation.2 | loop fusion | flops 2354688 | bytes 2377728 | tf_op jit(solution)/shard_map/reduce_sum | solution.py:21
  9.9 2.9 %fusion.3 = f32[48,96]{1,0:T(8,128)S(1)} fusion(bf16[48,96,256]{2,1,0:T(8,128)(2,1)} %param.12, f32[48,96]{1,0:T(8,128)S(1)} %broadcast_multiply_fusion), kind=kLoop, calls=%fused_computation.5 | loop fusion | flops 4713984 | bytes 2396160 | tf_op jit(solution)/shard_map/reduce_sum | solution.py:22
  12.8 0.0 copy-done.5
  12.8 0.0 copy-done.6
  12.8 2.9 %fusion.20 = bf16[8,48,96]{2,0,1:T(8,128)(2,1)S(1)} fusion(bf16[48,96,256]{2,1,0:T(8,128)(2,1)} %param.12, f32[256]{0:T(256)S(1)} %copy-done.5, f32[48,96]{1,0:T(8,128)S(1)} %add_rsqrt_fusion, f32[48,96]{1,0:T(8,128)S(1)} %broadcast_multiply_fusion, bf16[256,8]{0,1:T(8,128)(2,1)S(1)} %copy-done.6), kind=kOutput, calls=%fused_computation.25 | convolution fusion | flops 24809472 | bytes 2475008 | tf_op jit(solution)/shard_map/rcd,dh->hrc/dot_general | solution.py:144
  15.7 0.2 copy.26
  15.9 21.7 %all_gather.9 = bf16[8,48,384]{1,0,2:T(8,128)(2,1)} all-gather(bf16[8,48,96]{1,0,2:T(8,128)(2,1)S(1)} %copy.26), channel_id=1, replica_groups=mesh['row'=8,'col'=4] {'col'}, dimensions={2}, use_global_device_ids=true | all-gather | bytes 368640 | tf_op jit(solution)/shard_map/all_gather | solution.py:147
  37.6 0.0 all-gather.3.cloned.1.call-update
  37.6 3.6 %all-to-all-start = ((bf16[48,96,256]{2,1,0:T(8,128)(2,1)}), bf16[48,96,256]{2,1,0:T(8,128)(2,1)S(1)}, u32[]{:S(2)}, u32[]{:S(2)}) async-start(bf16[48,96,256]{2,1,0:T(8,128)(2,1)} %param.12), calls=%async_computation | async-start | bytes 4718592 | tf_op jit(solution)/shard_map/all_to_all | solution.py:149
  41.9 50.8 %all-to-all-done = bf16[48,96,256]{2,1,0:T(8,128)(2,1)S(1)} async-done(((bf16[48,96,256]{2,1,0:T(8,128)(2,1)}), bf16[48,96,256]{2,1,0:T(8,128)(2,1)S(1)}, u32[]{:S(2)}, u32[]{:S(2)}) %all-to-all-start) | async-done | bytes 2359328 | tf_op jit(solution)/shard_map/all_to_all | solution.py:149
  92.7 1.6 copy.25
  94.3 8.9 %copy.27 = bf16[64,48,384]{2,1,0:T(8,128)(2,1)} copy(bf16[64,48,384]{1,0,2:T(8,128)(2,1)} %all-gather.3.cloned.1.call-done) | data formatting | bytes 4718592 | tf_op jit(solution)/shard_map/all_gather | solution.py:148
  103.2 45.4 %slab_attention.1 = (bf16[12,384,256]{2,1,0:T(8,128)(2,1)}, bf16[12,16,384]{2,1,0:T(8,128)(2,1)}) custom-call(s32[1]{0:T(128)} %copy.41.length_ref, bf16[12,384,256]{2,1,0:T(8,128)(2,1)} %bitcast.55, bf16[8,8,48,384]{3,2,1,0:T(8,128)(2,1)} %bitcast.56, f32[1,256]{1,0:T(1,128)} %bitcast.65, bf16[4,256,256]{2,1,0:T(8,128)(2,1)} %proj_ref.1, ...), custom_call_target="tpu_custom_call" | custom-call | tf_op jit(solution)/shard_map/slab_attention/pallas_call | solution.py:99
  148.6 1.6 copy.31
  150.2 3.4 %all-to-all-start.2 = ((bf16[12,16,384]{2,0,1:T(8,128)(2,1)}), bf16[12,16,384]{2,0,1:T(8,128)(2,1)S(1)}, u32[]{:S(2)}, u32[]{:S(2)}) async-start(bf16[12,16,384]{2,0,1:T(8,128)(2,1)} %copy.31), calls=%async_computation.2 | async-start | bytes 393216 | tf_op jit(solution)/shard_map/all_to_all | solution.py:161
  153.6 4.7 %copy.28 = bf16[12,384,256]{2,0,1:T(8,128)(2,1)} copy(bf16[12,384,256]{2,1,0:T(8,128)(2,1)} %get-tuple-element.4) | data formatting | bytes 4718592 | tf_op jit(solution)/shard_map/slab_attention/pallas_call | solution.py:99
  158.3 2.5 %all-to-all-done.2 = bf16[12,16,384]{2,0,1:T(8,128)(2,1)S(1)} async-done(((bf16[12,16,384]{2,0,1:T(8,128)(2,1)}), bf16[12,16,384]{2,0,1:T(8,128)(2,1)S(1)}, u32[]{:S(2)}, u32[]{:S(2)}) %all-to-all-start.2) | async-done | bytes 147488 | tf_op jit(solution)/shard_map/all_to_all | solution.py:161
  160.8 0.7 copy-done.2
  161.5 3.7 %all-to-all-start.1 = ((bf16[12,384,256]{2,0,1:T(8,128)(2,1)}), bf16[12,384,256]{2,0,1:T(8,128)(2,1)S(1)}, u32[]{:S(2)}, u32[]{:S(2)}) async-start(bf16[12,384,256]{2,0,1:T(8,128)(2,1)} %copy.28), calls=%async_computation.1 | async-start | bytes 6291456 | tf_op jit(solution)/shard_map/all_to_all | solution.py:160
  165.2 0.2 reduce-scatter.4.cloned.1.call-start
  165.5 1.2 convert_reduce_fusion.1
  166.7 1.4 fusion.11
  168.1 0.0 copy-done.4
  168.1 1.3 fusion.13
  169.4 0.0 copy-start.3
  169.4 0.8 copy-done.3
  170.2 1.1 convolution_convert_fusion.3
  171.3 0.1 reshape.49
  171.5 1.5 convolution_convert_fusion
  173.0 2.2 convolution_convert_fusion.1
  175.2 1.0 copy.32
  176.2 0.2 fusion.15
  176.4 0.7 copy-done.1
  177.1 0.2 fusion.50
  177.3 1.5 fusion.38
  178.8 0.7 copy.35
  179.5 1.4 convolution_convert_fusion.2
  180.9 0.8 copy.36
  181.8 0.0 reduce-scatter.4.cloned.1.call-update
  181.8 39.7 %reduce-scatter.4.cloned.1.call-done = bf16[192,48]{1,0:T(8,128)(2,1)} async-done(((bf16[768,48]{1,0:T(8,128)(2,1)}), bf16[192,48]{1,0:T(8,128)(2,1)}) %reduce-scatter.4.cloned.1.call-update) | async-done | bytes 18448
  221.4 0.9 copy.37
  222.3 1.5 add_convert_fusion
  223.8 13.2 %all-to-all-done.1 = bf16[12,384,256]{2,0,1:T(8,128)(2,1)S(1)} async-done(((bf16[12,384,256]{2,0,1:T(8,128)(2,1)}), bf16[12,384,256]{2,0,1:T(8,128)(2,1)S(1)}, u32[]{:S(2)}, u32[]{:S(2)}) %all-to-all-start.1) | async-done | bytes 2359328 | tf_op jit(solution)/shard_map/all_to_all | solution.py:160
  237.0 2.3 copy.29
  (10 shorter events, 0.0 us)
Async XLA Ops:
  7.2 172.4 %copy-start = (bf16[192,768]{1,0:T(8,128)(2,1)S(1)}, bf16[192,768]{1,0:T(8,128)(2,1)}, u32[]{:S(2)}) copy-start(bf16[192,768]{1,0:T(8,128)(2,1)} %param.23) | copy-start | bytes 884740
  7.2 5.6 %copy-start.5 = (f32[256]{0:T(256)S(1)}, f32[256]{0:T(256)}, u32[]{:S(2)}) copy-start(f32[256]{0:T(256)} %param.15) | copy-start | bytes 3076
  7.2 5.6 %copy-start.6 = (bf16[256,8]{0,1:T(8,128)(2,1)S(1)}, bf16[256,8]{0,1:T(8,128)(2,1)}, u32[]{:S(2)}) copy-start(bf16[256,8]{0,1:T(8,128)(2,1)} %param.17) | copy-start | bytes 12292
  7.2 87.1 %all-gather.3.cloned.1.call-start = ((), (), s32[]{:S(2)}) async-start(), calls=%async_computation.4 | async-start | bytes 7077888 | tf_op jit(solution)/shard_map/all_gather | solution.py:148
  37.6 55.1 %all-to-all-start = ((bf16[48,96,256]{2,1,0:T(8,128)(2,1)}), bf16[48,96,256]{2,1,0:T(8,128)(2,1)S(1)}, u32[]{:S(2)}, u32[]{:S(2)}) async-start(bf16[48,96,256]{2,1,0:T(8,128)(2,1)} %param.12), calls=%async_computation | async-start | bytes 4718592 | tf_op jit(solution)/shard_map/all_to_all | solution.py:149
  150.2 10.6 %all-to-all-start.2 = ((bf16[12,16,384]{2,0,1:T(8,128)(2,1)}), bf16[12,16,384]{2,0,1:T(8,128)(2,1)S(1)}, u32[]{:S(2)}, u32[]{:S(2)}) async-start(bf16[12,16,384]{2,0,1:T(8,128)(2,1)} %copy.31), calls=%async_computation.2 | async-start | bytes 393216 | tf_op jit(solution)/shard_map/all_to_all | solution.py:161
  158.3 9.8 %copy-start.4 = (f32[768]{0:T(1024)S(1)}, f32[768]{0:T(1024)}, u32[]{:S(2)}) copy-start(f32[768]{0:T(1024)} %param.19) | copy-start | bytes 9220
  160.8 0.7 copy-start.2
  161.5 75.4 %all-to-all-start.1 = ((bf16[12,384,256]{2,0,1:T(8,128)(2,1)}), bf16[12,384,256]{2,0,1:T(8,128)(2,1)S(1)}, u32[]{:S(2)}, u32[]{:S(2)}) async-start(bf16[12,384,256]{2,0,1:T(8,128)(2,1)} %copy.28), calls=%async_computation.1 | async-start | bytes 6291456 | tf_op jit(solution)/shard_map/all_to_all | solution.py:160
  165.2 56.2 %reduce-scatter.4.cloned.1.call-start = ((), (), s32[]{:S(2)}) async-start(), calls=%async_computation.5 | async-start | bytes 245760
  169.4 0.8 copy-start.3
  176.4 0.7 copy-start.1
Sparse Core Ops, SparseCore 0:
  37.7 46.2 all-gather.2
  181.9 39.4 reduce-scatter.3

commit v2 on v1

v2 whole, which is shorter than its diff:
```python
import math

import jax
import jax.numpy as jnp
from jax import lax
from jax.experimental import pallas as pl
from jax.experimental.pallas import tpu as pltpu
from jax.sharding import PartitionSpec as P

PAIR_HEADS = 8
PAIR_HEAD_DIM = 32
SINGLE_HEAD_DIM = 48
LOG2E = math.log2(math.e)

masked_value = -1e30
NT = (((1,), (1,)), ((), ()))


def normalize(values, scales):
    floated = values.astype(jnp.float32)
    center = jnp.mean(floated, axis=-1, keepdims=True)
    spread = jnp.mean(jnp.square(floated - center), axis=-1, keepdims=True)
    return ((floated - center) * lax.rsqrt(spread + 1e-05) * scales).astype(jnp.bfloat16)


def project(inputs, matrix):
    return jnp.dot(inputs, matrix, preferred_element_type=jnp.float32).astype(jnp.bfloat16)


def row_update(rep, gain, proj_ref, out_weight, bias_of):
    channels = rep.shape[1]
    half = channels // 2
    heads_per_half = PAIR_HEADS // 2
    normed = normalize(rep, gain)
    f32 = jnp.float32
    query = jnp.dot(normed, proj_ref[0], preferred_element_type=f32)
    query = (query * (LOG2E / math.sqrt(PAIR_HEAD_DIM))).astype(jnp.bfloat16)
    key = project(normed, proj_ref[1])
    value = project(normed, proj_ref[2])
    gate = jax.nn.sigmoid(jnp.dot(normed, proj_ref[3], preferred_element_type=f32))
    head_of_lane = lax.broadcasted_iota(jnp.int32, (1, half), 1) // PAIR_HEAD_DIM
    halves = []
    for side in range(2):
        span = slice(side * half, (side + 1) * half)
        q_half, k_half, v_half = query[:, span], key[:, span], value[:, span]
        top = bottom = None
        for sub in range(heads_per_half):
            head = side * heads_per_half + sub
            mine = head_of_lane == sub
            q_head = jnp.where(mine, q_half, jnp.zeros_like(q_half))
            scores = lax.dot_general(q_head, k_half, NT, preferred_element_type=f32)
            scores = scores + bias_of(head)
            peak = jnp.max(scores, axis=-1, keepdims=True)
            exponent = jnp.exp2(scores - peak).astype(jnp.bfloat16)
            v_ext = jnp.concatenate([v_half, jnp.ones_like(v_half)], axis=1)
            both = jnp.dot(exponent, v_ext, preferred_element_type=f32)
            num, den = both[:, :half], both[:, half:]
            top = num if top is None else jnp.where(mine, num, top)
            bottom = den if bottom is None else jnp.where(mine, den, bottom)
        halves.append(top / bottom)
    attended = jnp.concatenate(halves, axis=1)
    hidden = (gate * attended).astype(jnp.bfloat16)
    return (
        rep.astype(f32) + jnp.dot(hidden, out_weight, preferred_element_type=f32)
    ).astype(jnp.bfloat16)


def slot(ref, *index):
    return ref.at[index]


def window_kernel(
    length_ref, pair_ref, tri_ref, single_ref, rest_ref, gain_ref, proj_ref, out_weight_ref,
    bias_gain_ref, head_weight_ref, single_gain_ref, single_proj_ref, single_out_ref,
    pair_out_ref, single_new_ref,
    slab, fresh, bands, bias_held, head_kept, head_sent, head_got, head_full,
    s_query, s_key, s_value, s_gate, part_sent, part_got,
    in_send, in_recv, in_own, out_send, out_recv, out_own,
    col_send, col_recv, col_own, chip_send, chip_recv, core_send, core_recv,
    head_send, head_recv, part_send, part_recv,
):
    f32 = jnp.float32
    slab_rows, cols, cols_here, channels = slab.shape
    rows, _, heads, rows_here, _ = bands.shape
    tokens = cols * cols_here
    chips = rows // 2
    row, col = lax.axis_index("row"), lax.axis_index("col")
    chip, core = row // 2, lax.rem(row, 2)
    partner = chip * 2 + 1 - core
    mesh_id = pl.DeviceIdType.MESH

    def peer(step):
        return lax.rem(col + step, cols)

    def chip_row(step):
        return lax.rem(chip + step, chips) * 2 + core

    def chip_back(step):
        return lax.rem(chip + chips - step, chips) * 2 + core

    barrier = pltpu.get_barrier_semaphore()
    for step in range(1, cols):
        pl.semaphore_signal(barrier, inc=1, device_id=(row, peer(step)), device_id_type=mesh_id)
    for step in range(1, chips):
        pl.semaphore_signal(barrier, inc=1, device_id=(chip_row(step), col), device_id_type=mesh_id)
    pl.semaphore_signal(barrier, inc=1, device_id=(partner, col), device_id_type=mesh_id)
    pl.semaphore_wait(barrier, cols + chips - 1)

    def remote(src, dst, send, recv, to):
        return pltpu.make_async_remote_copy(
            src_ref=src, dst_ref=dst, send_sem=send, recv_sem=recv,
            device_id=to, device_id_type=mesh_id,
        )

    def col_copy(step):
        return remote(
            tri_ref, slot(bands, row, col), col_send.at[step], col_recv.at[step], (row, peer(step))
        )

    def chip_copy(step):
        return remote(
            slot(bands, row), slot(bands, row), chip_send.at[step], chip_recv.at[step],
            (chip_row(step), col),
        )

    def core_copy(step):
        band = chip_back(step)
        return remote(
            slot(bands, band), slot(bands, band), core_send.at[step], core_recv.at[step],
            (partner, col),
        )

    def in_copy(s, step):
        to = peer(step)
        return remote(
            slot(pair_ref, to * slab_rows + s), slot(slab, s, col),
            in_send.at[s, step], in_recv.at[s, step], (row, to),
        )

    def own_in(s):
        return pltpu.make_async_copy(
            slot(pair_ref, col * slab_rows + s), slot(slab, s, col), in_own.at[s]
        )

    def out_copy(s, step):
        to = peer(step)
        return remote(
            slot(fresh, s, to), slot(pair_out_ref, col * slab_rows + s),
            out_send.at[s, step], out_recv.at[s, step], (row, to),
        )

    def own_out(s):
        return pltpu.make_async_copy(
            slot(fresh, s, col), slot(pair_out_ref, col * slab_rows + s), out_own.at[s]
        )

    def head_copy(step):
        to = peer(step)
        return remote(
            slot(head_sent, to), slot(head_got, col), head_send.at[step], head_recv.at[step],
            (row, to),
        )

    def part_copy(step):
        to = peer(step)
        return remote(
            slot(part_sent, to), slot(part_got, step), part_send.at[step], part_recv.at[step],
            (row, to),
        )

    for step in range(1, cols):
        col_copy(step).start()
    own_block = pltpu.make_async_copy(tri_ref, slot(bands, row, col), col_own)
    own_block.start()

    @pl.loop(0, slab_rows)
    def _(s):
        own_in(s).start()
        for step in range(1, cols):
            in_copy(s, step).start()

    for step in range(1, cols):
        col_copy(step).wait_recv()
    own_block.wait()
    for step in range(1, chips):
        chip_copy(step).start()
    core_copy(0).start()

    s_normed = normalize(single_ref[...], single_gain_ref[...])
    s_key[...] = project(s_normed, single_proj_ref[1])
    s_value[...] = project(s_normed, single_proj_ref[2])
    mine = normalize(
        single_ref[pl.ds(pl.multiple_of(row * rows_here, rows_here), rows_here), :],
        single_gain_ref[...],
    )
    s_query[...] = (
        jnp.dot(mine, single_proj_ref[0], preferred_element_type=f32)
        * (LOG2E / math.sqrt(SINGLE_HEAD_DIM))
    ).astype(jnp.bfloat16)
    s_gate[...] = jax.nn.sigmoid(jnp.dot(mine, single_proj_ref[3], preferred_element_type=f32))

    def take_band(band):
        start = pl.multiple_of(band * rows_here, rows_here)
        for part in range(cols):
            usable = (
                lax.broadcasted_iota(jnp.int32, (1, 1, cols_here), 2) + part * cols_here
                < length_ref[0]
            )
            piece = bands[band, part].astype(f32) * LOG2E
            bias_held[:, pl.ds(start, rows_here), part * cols_here : (part + 1) * cols_here] = (
                jnp.where(usable, piece, masked_value)
            )

    take_band(row)
    for step in range(1, chips):
        chip_copy(step).wait_recv()
        core_copy(step).start()
        take_band(chip_back(step))
    for step in range(chips):
        core_copy(step).wait_recv()
        take_band(chip_back(step) + 1 - 2 * core)

    early = slab_rows // 2

    def one_row(s):
        own_in(s).wait()
        for step in range(1, cols):
            in_copy(s, step).wait_recv()
        rep = slab[s].reshape(tokens, channels)
        updated = row_update(
            rep, gain_ref[...], proj_ref, out_weight_ref[...], lambda head: bias_held[head]
        )
        fresh[s] = updated.reshape(cols, cols_here, channels)
        again = normalize(updated, bias_gain_ref[...])
        head_kept[:, s, :] = lax.dot_general(
            head_weight_ref[...], again, NT, preferred_element_type=f32
        )

    def send_row(s):
        own_out(s).start()
        for step in range(1, cols):
            out_copy(s, step).start()

    @pl.loop(0, slab_rows)
    def _(s):
        one_row(s)

        @pl.when(s < early)
        def _():
            send_row(s)

    head_sent[...] = head_kept[...].astype(jnp.bfloat16).reshape(head_sent.shape)
    for step in range(1, cols):
        head_copy(step).start()

    @pl.loop(early, slab_rows)
    def _(s):
        send_row(s)

    for step in range(1, cols):
        head_copy(step).wait_recv()
    for part in range(cols):
        span = slice(part * slab_rows, (part + 1) * slab_rows)

        @pl.when(col == part)
        def _():
            head_full[:, span, :] = head_sent[part].astype(f32) * LOG2E

        @pl.when(col != part)
        def _():
            head_full[:, span, :] = head_got[part].astype(f32) * LOG2E

    width = s_key.shape[1]
    s_heads = head_full.shape[0]
    usable = lax.broadcasted_iota(jnp.int32, (1, tokens), 1) < length_ref[0]
    head_of_lane = lax.broadcasted_iota(jnp.int32, (1, width), 1) // SINGLE_HEAD_DIM
    blended = jnp.zeros((rows_here, width), f32)
    for head in range(s_heads):
        here = head_of_lane == head
        q_head = jnp.where(here, s_query[...], jnp.zeros_like(s_query[...]))
        scores = lax.dot_general(q_head, s_key[...], NT, preferred_element_type=f32)
        scores = jnp.where(usable, scores + head_full[head], masked_value)
        exponent = jnp.exp2(scores - jnp.max(scores, axis=-1, keepdims=True))
        total = jnp.sum(exponent, axis=-1, keepdims=True)
        weights = (exponent / total).astype(jnp.bfloat16)
        blended = jnp.where(
            here, jnp.dot(weights, s_value[...], preferred_element_type=f32), blended
        )
    s_hidden = (s_gate[...] * blended).astype(jnp.bfloat16)
    for part in range(cols):
        share = jnp.dot(s_hidden, single_out_ref[part], preferred_element_type=f32)
        part_sent[part] = share.astype(jnp.bfloat16)
    for step in range(1, cols):
        part_copy(step).start()
    total = rest_ref[...].astype(f32) + part_sent[col].astype(f32)
    for step in range(1, cols):
        part_copy(step).wait_recv()
        total = total + part_got[step].astype(f32)
    single_new_ref[...] = total.astype(jnp.bfloat16)

    for step in range(1, cols):
        col_copy(step).wait_send()
        head_copy(step).wait_send()
        part_copy(step).wait_send()
    for step in range(1, chips):
        chip_copy(step).wait_send()
    for step in range(chips):
        core_copy(step).wait_send()

    @pl.loop(0, slab_rows)
    def _(s):
        own_out(s).wait()
        for step in range(1, cols):
            in_copy(s, step).wait_send()
            out_copy(s, step).wait_send()
            out_copy(s, step).wait_recv()


def per_device(
    pair_rep,
    single_rep,
    length,
    pair_gain,
    pair_proj,
    bias_weight,
    pair_out_weight,
    single_gain,
    single_proj,
    bias_norm_gain,
    single_bias_weight,
    single_out_weight,
):
    rows_here, cols_here, channels = pair_rep.shape
    rows, cols = lax.axis_size("row"), lax.axis_size("col")
    tokens = rows_here * rows
    slab_rows = rows_here // cols
    chips = rows // 2
    heads = bias_weight.shape[1]
    single_heads = single_bias_weight.shape[1]
    heads_here = single_heads // cols
    width = single_proj.shape[2]
    normed = normalize(pair_rep, pair_gain)
    local_bias = jnp.einsum(
        "rcd,dh->hrc", normed, bias_weight, preferred_element_type=jnp.float32
    ).astype(jnp.bfloat16)
    row_start = lax.axis_index("row") * rows_here
    col_start = lax.axis_index("col") * width
    residual = lax.dynamic_slice(single_rep, (row_start, col_start), (rows_here, width))
    out_pieces = single_out_weight.reshape(width, cols, width).transpose(1, 0, 2)
    bf16, f32 = jnp.bfloat16, jnp.float32
    dma = pltpu.SemaphoreType.DMA
    anywhere = pl.BlockSpec(memory_space=pl.ANY)
    held = pl.BlockSpec(memory_space=pltpu.VMEM)
    pair_out, single_out = pl.pallas_call(
        window_kernel,
        in_specs=[pl.BlockSpec(memory_space=pltpu.SMEM), anywhere] + [held] * 11,
        out_specs=[anywhere, held],
        out_shape=[
            jax.ShapeDtypeStruct(pair_rep.shape, bf16),
            jax.ShapeDtypeStruct((rows_here, width), bf16),
        ],
        scratch_shapes=[
            pltpu.VMEM((slab_rows, cols, cols_here, channels), bf16),
            pltpu.VMEM((slab_rows, cols, cols_here, channels), bf16),
            pltpu.VMEM((rows, cols, heads, rows_here, cols_here), bf16),
            pltpu.VMEM((heads, tokens, tokens), f32),
            pltpu.VMEM((single_heads, slab_rows, tokens), f32),
            pltpu.VMEM((cols, heads_here, slab_rows, tokens), bf16),
            pltpu.VMEM((cols, heads_here, slab_rows, tokens), bf16),
            pltpu.VMEM((heads_here, rows_here, tokens), f32),
            pltpu.VMEM((rows_here, width), bf16),
            pltpu.VMEM((tokens, width), bf16),
            pltpu.VMEM((tokens, width), bf16),
            pltpu.VMEM((rows_here, width), f32),
            pltpu.VMEM((cols, rows_here, width), bf16),
            pltpu.VMEM((cols, rows_here, width), bf16),
            dma((slab_rows, cols)),
            dma((slab_rows, cols)),
            dma((slab_rows,)),
            dma((slab_rows, cols)),
            dma((slab_rows, cols)),
            dma((slab_rows,)),
            dma((cols,)),
            dma((cols,)),
            dma,
            dma((chips,)),
            dma((chips,)),
            dma((chips,)),
            dma((chips,)),
            dma((cols,)),
            dma((cols,)),
            dma((cols,)),
            dma((cols,)),
        ],
        compiler_params=pltpu.CompilerParams(
            collective_id=0, has_side_effects=True, vmem_limit_bytes=60 * 2**20
        ),
        name="window",
    )(
        length, pair_rep, local_bias, single_rep, residual, pair_gain[None], pair_proj,
        pair_out_weight, bias_norm_gain[None], single_bias_weight.T, single_gain[None],
        single_proj, out_pieces,
    )
    return (pair_out, single_out)


def solution(mesh):
    in_specs = (
        P("row", "col", None),
        P(),
        P(),
        P(),
        P(),
        P(),
        P(),
        P(),
        P(None, None, "col"),
        P(),
        P(),
        P("col", None),
    )
    out_specs = (P("row", "col", None), P("row", "col"))
    return jax.shard_map(
        per_device, mesh=mesh, in_specs=in_specs, out_specs=out_specs, check_vma=False
    )
```

time: 247 us -> 147 us (0.60)
  waiting for transfers between devices: 106 us -> 0 us
  Pallas kernels: 45.4 us -> 128 us
  blocking collectives: 21.7 us -> 0 us
  local copies, waits for them, and re-layouts: 25.1 us -> 10.9 us
  between operations: 14.9 us -> 1.54 us
  starting transfers between devices: 11 us -> 0 us
  matrix products: 10.8 us -> 1.99 us
  other arithmetic: 11.1 us -> 4.23 us
    pallas_call x1, Pallas kernels: 45.4 us -> 128 us  [per_device(): pl.pallas_call(window_kernel, in_specs=[pl.BlockSpec(memory_space=pltpu.S...]
    all_to_all x3 -> x0, waiting for transfers between devices: 66.5 us -> none  [the longest x1 50.8 us: per_device(): lax.all_to_all(pair_rep, 'col', split_axis=0, concat_axis=1, tiled=True)]
    unnamed x3 -> x0, waiting for transfers between devices: 39.7 us -> none
    all_gather x1 -> x0, blocking collectives: 21.7 us -> none  [per_device(): row_band = lax.all_gather(local_bias, 'col', axis=2, tiled=True)]
    all_to_all x3 -> x0, starting transfers between devices: 10.7 us -> none  [the longest x1 3.7 us: per_device(): lax.all_to_all(updated_slab, 'col', split_axis=1, concat_axis=0, tiled=True)]
    all_gather x1 -> x0, local copies, waits for them, and re-layouts: 8.92 us -> none  [per_device(): bias_bands = lax.all_gather(row_band, 'row')]
    dot_general x6 -> x0, matrix products: 7.93 us -> none  [the longest x3 4.84 us: project(): jnp.dot(inputs, matrix, preferred_element_type=jnp.float32)]
    pallas_call x2 -> x0, local copies, waits for them, and re-layouts: 6.37 us -> none  [slab_attention(): pl.pallas_call(slab_kernel, grid=(rows,), in_specs=[pl.BlockSpec(memory_s...]
  transfers between devices with their start and end apart: 5 -> 0, of which waited for: 4 -> 0; matrix products, arithmetic and copies ran while one was open for 10% -> 0% of each run, Pallas kernels for 0% -> 0%
where the time goes in v2:
time: 147 us; the launch traced here: 146 us
  Pallas kernels  128 us (87%)
  local copies, waits for them, and re-layouts  10.9 us (7%)
  other arithmetic  4.23 us (3%)
  matrix products  1.99 us (1%)
  between operations  1.54 us (1%)
    pallas_call x1, Pallas kernels, per_device(): pl.pallas_call(window_kernel, in_specs=[pl.BlockSpec(memory_space=pltpu.S...  128 us
    unnamed x13, local copies, waits for them, and re-layouts  5.4 us

profile of v2, /device:TPU:0, one launch (start us, length us, event | category | flops | bytes accessed | tf_op | source)
XLA Modules:
  0.0 146.4 jit_solution(3870114287449238046)
XLA Ops:
  0.6 0.0 copy-start
  0.6 0.0 copy-start.1
  1.5 1.3 broadcast_in_dim.14.single_gain_ref
  2.7 1.5 dynamic_slice.3.rest_ref
  4.2 0.0 copy-start.4
  4.2 2.6 %convert_reduce_fusion = f32[48,96]{1,0:T(8,128)S(1)} fusion(bf16[48,96,256]{2,1,0:T(8,128)(2,1)} %pair_ref.1), kind=kLoop, calls=%fused_computation.1 | loop fusion | flops 2354688 | bytes 2377728 | tf_op jit(solution)/shard_map/reduce_sum | solution.py:21
  6.8 0.0 copy-done.1
  6.8 1.7 %fusion.2 = f32[48,96]{1,0:T(8,128)S(1)} fusion(bf16[48,96,256]{2,1,0:T(8,128)(2,1)S(1)} %copy-done.1, f32[48,96]{1,0:T(8,128)S(1)} %broadcast_multiply_fusion), kind=kLoop, calls=%fused_computation.4 | loop fusion | flops 4713984 | bytes 2396160 | tf_op jit(solution)/shard_map/reduce_sum | solution.py:22
  8.5 0.0 copy-done
  8.5 0.0 copy-done.4
  8.5 0.0 copy-start.2
  8.5 2.0 %fusion.5 = bf16[48,96,8]{1,2,0:T(8,128)(2,1)S(1)} fusion(bf16[48,96,256]{2,1,0:T(8,128)(2,1)S(1)} %copy-done.1, f32[256]{0:T(256)S(1)} %copy-done.4, f32[48,96]{1,0:T(8,128)S(1)} %add_rsqrt_fusion, f32[48,96]{1,0:T(8,128)S(1)} %broadcast_multiply_fusion, bf16[256,8]{0,1:T(8,128)(2,1)S(1)} %copy-done), kind=kOutput, calls=%fused_computation.7 | convolution fusion | flops 24772608 | bytes 2475008 | tf_op jit(solution)/shard_map/rcd,dh->hrc/dot_general | solution.py:343
  10.5 0.7 copy.24
  11.2 1.3 reshape.20
  12.5 0.8 copy.23
  13.3 0.0 copy-done.2
  13.3 1.5 %copy.18.single_proj_ref = bf16[4,768,192]{2,1,0:T(8,128)(2,1)} copy(bf16[4,768,192]{1,2,0:T(8,128)(2,1)S(1)} %copy-done.2) | data formatting | bytes 2359296 | tf_op args[8]
  14.8 127.7 %window.1 = (bf16[48,96,256]{2,1,0:T(8,128)(2,1)}, bf16[48,192]{1,0:T(8,128)(2,1)}) custom-call(s32[1]{0:T(128)S(6)} %copy.27.length_ref, bf16[48,96,256]{2,1,0:T(8,128)(2,1)} %pair_ref.1, bf16[8,48,96]{2,1,0:T(8,128)(2,1)} %bitcast.13, bf16[384,768]{1,0:T(8,128)(2,1)} %single_ref.1, bf16[48,192]{1,0:T(8,128)(2,1)} %dynamic_slice.3.rest_ref, ...), custom_call_target="tpu_custom_call" | custom-call | tf_op jit(solution)/shard_map/window/pallas_call | solution.py:354
  142.5 0.0 copy-start.3
  142.5 3.2 %copy.28 = bf16[48,96,256]{2,1,0:T(8,128)(2,1)} copy(bf16[48,96,256]{2,1,0:T(8,128)(2,1)} %get-tuple-element.4) | data formatting | bytes 4718592
  145.8 0.0 copy-done.3
  145.8 0.6 copy.29
  (2 shorter events, 0.0 us)
Async XLA Ops:
  0.6 7.8 %copy-start = (bf16[256,8]{0,1:T(8,128)(2,1)S(1)}, bf16[256,8]{0,1:T(8,128)(2,1)}, u32[]{:S(2)}) copy-start(bf16[256,8]{0,1:T(8,128)(2,1)} %param.17) | copy-start | bytes 12292
  0.6 6.1 %copy-start.1 = (bf16[48,96,256]{2,1,0:T(8,128)(2,1)S(1)}, bf16[48,96,256]{2,1,0:T(8,128)(2,1)}, u32[]{:S(2)}) copy-start(bf16[48,96,256]{2,1,0:T(8,128)(2,1)} %pair_ref.1) | copy-start | bytes 7077892
  4.2 4.3 %copy-start.4 = (f32[256]{0:T(256)S(1)}, f32[256]{0:T(256)}, u32[]{:S(2)}) copy-start(f32[256]{0:T(256)} %param.15) | copy-start | bytes 3076
  8.5 4.8 %copy-start.2 = (bf16[4,768,192]{1,2,0:T(8,128)(2,1)S(1)}, bf16[4,768,192]{1,2,0:T(8,128)(2,1)}, u32[]{:S(2)}) copy-start(bf16[4,768,192]{1,2,0:T(8,128)(2,1)} %param.20) | copy-start | bytes 3538948
  142.5 3.2 %copy-start.3 = (bf16[48,192]{1,0:T(8,128)(2,1)S(1)}, bf16[48,192]{1,0:T(8,128)(2,1)}, u32[]{:S(2)}) copy-start(bf16[48,192]{1,0:T(8,128)(2,1)} %get-tuple-element.5) | copy-start | bytes 55300

commit v3 on v2

--- a/solution.py
+++ b/solution.py
@@ -25,6 +25,12 @@
 
 def project(inputs, matrix):
     return jnp.dot(inputs, matrix, preferred_element_type=jnp.float32).astype(jnp.bfloat16)
+
+
+def project_t(inputs, matrix):
+    return lax.dot_general(inputs, matrix, NT, preferred_element_type=jnp.float32).astype(
+        jnp.bfloat16
+    )
 
 
 def row_update(rep, gain, proj_ref, out_weight, bias_of):
@@ -70,9 +76,11 @@
 
 
 def window_kernel(
-    length_ref, pair_ref, tri_ref, single_ref, rest_ref, gain_ref, proj_ref, out_weight_ref,
-    bias_gain_ref, head_weight_ref, single_gain_ref, single_proj_ref, single_out_ref,
+    length_ref, pair_ref, single_hbm, proj_hbm, out_weight_hbm, single_proj_hbm, single_out_hbm,
+    gain_ref, tri_weight_ref, bias_gain_ref, head_weight_ref, single_gain_ref,
     pair_out_ref, single_new_ref,
+    local, tri_kept, tri_ref, single_ref, proj_ref, out_weight_ref, single_proj_ref, single_out_ref,
+    rest_ref, local_sem, weight_sem,
     slab, fresh, bands, bias_held, head_kept, head_sent, head_got, head_full,
     s_query, s_key, s_value, s_gate, part_sent, part_got,
     in_send, in_recv, in_own, out_send, out_recv, out_own,
@@ -98,6 +106,27 @@
     def chip_back(step):
         return lax.rem(chip + chips - step, chips) * 2 + core
 
+    def local_copy(part):
+        span = pl.ds(part * slab_rows, slab_rows)
+        return pltpu.make_async_copy(pair_ref.at[span], local.at[span], local_sem.at[part])
+
+    weight_copies = [
+        pltpu.make_async_copy(src, dst, weight_sem.at[i])
+        for i, (src, dst) in enumerate(
+            (
+                (single_hbm, single_ref),
+                (single_proj_hbm, single_proj_ref),
+                (proj_hbm, proj_ref),
+                (out_weight_hbm, out_weight_ref),
+                (single_out_hbm, single_out_ref),
+            )
+        )
+    ]
+    for part in range(cols):
+        local_copy(part).start()
+    for copy in weight_copies:
+        copy.start()
+
     barrier = pltpu.get_barrier_semaphore()
     for step in range(1, cols):
         pl.semaphore_signal(barrier, inc=1, device_id=(row, peer(step)), device_id_type=mesh_id)
@@ -168,16 +197,37 @@
             (row, to),
         )
 
+    def bring_row(s):
+        own_in(s).start()
+        for step in range(1, cols):
+            in_copy(s, step).start()
+
+    bring_row(0)
+    group = math.gcd(slab_rows, 6)
+    for part in range(cols):
+        local_copy(part).wait()
+
+        @pl.loop(0, slab_rows // group)
+        def _(i):
+            for j in range(group):
+                r = part * slab_rows + i * group + j
+                tri_kept[:, r, :] = lax.dot_general(
+                    tri_weight_ref[...], normalize(local[r], gain_ref[...]), NT,
+                    preferred_element_type=f32,
+                )
+
+    tri_ref[...] = tri_kept[...].astype(jnp.bfloat16)
     for step in range(1, cols):
         col_copy(step).start()
     own_block = pltpu.make_async_copy(tri_ref, slot(bands, row, col), col_own)
     own_block.start()
 
-    @pl.loop(0, slab_rows)
+    @pl.loop(1, slab_rows)
     def _(s):
-        own_in(s).start()
-        for step in range(1, cols):
-            in_copy(s, step).start()
+        bring_row(s)
+
+    for copy in weight_copies:
+        copy.wait()
 
     for step in range(1, cols):
         col_copy(step).wait_recv()
@@ -187,17 +237,27 @@
     core_copy(0).start()
 
     s_normed = normalize(single_ref[...], single_gain_ref[...])
-    s_key[...] = project(s_normed, single_proj_ref[1])
-    s_value[...] = project(s_normed, single_proj_ref[2])
+    s_key[...] = project_t(s_normed, single_proj_ref[1])
+    s_value[...] = project_t(s_normed, single_proj_ref[2])
+    width = s_key.shape[1]
+    my_rows = pl.ds(pl.multiple_of(row * rows_here, rows_here), rows_here)
+    for part in range(cols):
+
+        @pl.when(col == part)
+        def _():
+            rest_ref[...] = single_ref[my_rows, part * width : (part + 1) * width]
+
     mine = normalize(
-        single_ref[pl.ds(pl.multiple_of(row * rows_here, rows_here), rows_here), :],
+        single_ref[my_rows, :],
         single_gain_ref[...],
     )
     s_query[...] = (
-        jnp.dot(mine, single_proj_ref[0], preferred_element_type=f32)
+        lax.dot_general(mine, single_proj_ref[0], NT, preferred_element_type=f32)
         * (LOG2E / math.sqrt(SINGLE_HEAD_DIM))
     ).astype(jnp.bfloat16)
-    s_gate[...] = jax.nn.sigmoid(jnp.dot(mine, single_proj_ref[3], preferred_element_type=f32))
+    s_gate[...] = jax.nn.sigmoid(
+        lax.dot_general(mine, single_proj_ref[3], NT, preferred_element_type=f32)
+    )
 
     def take_band(band):
         start = pl.multiple_of(band * rows_here, rows_here)
@@ -220,7 +280,8 @@
         core_copy(step).wait_recv()
         take_band(chip_back(step) + 1 - 2 * core)
 
-    early = slab_rows // 2
+    early = 2 * slab_rows // 3
+    late = slab_rows - slab_rows // 6
 
     def one_row(s):
         own_in(s).wait()
@@ -253,7 +314,7 @@
     for step in range(1, cols):
         head_copy(step).start()
 
-    @pl.loop(early, slab_rows)
+    @pl.loop(early, late)
     def _(s):
         send_row(s)
 
@@ -270,7 +331,6 @@
         def _():
             head_full[:, span, :] = head_got[part].astype(f32) * LOG2E
 
-    width = s_key.shape[1]
     s_heads = head_full.shape[0]
     usable = lax.broadcasted_iota(jnp.int32, (1, tokens), 1) < length_ref[0]
     head_of_lane = lax.broadcasted_iota(jnp.int32, (1, width), 1) // SINGLE_HEAD_DIM
@@ -287,11 +347,16 @@
             here, jnp.dot(weights, s_value[...], preferred_element_type=f32), blended
         )
     s_hidden = (s_gate[...] * blended).astype(jnp.bfloat16)
+    share = jnp.dot(s_hidden, single_out_ref[...], preferred_element_type=f32)
     for part in range(cols):
-        share = jnp.dot(s_hidden, single_out_ref[part], preferred_element_type=f32)
-        part_sent[part] = share.astype(jnp.bfloat16)
+        part_sent[part] = share[:, part * width : (part + 1) * width].astype(jnp.bfloat16)
     for step in range(1, cols):
         part_copy(step).start()
+
+    @pl.loop(late, slab_rows)
+    def _(s):
+        send_row(s)
+
     total = rest_ref[...].astype(f32) + part_sent[col].astype(f32)
     for step in range(1, cols):
         part_copy(step).wait_recv()
@@ -339,27 +404,31 @@
     single_heads = single_bias_weight.shape[1]
     heads_here = single_heads // cols
     width = single_proj.shape[2]
-    normed = normalize(pair_rep, pair_gain)
-    local_bias = jnp.einsum(
-        "rcd,dh->hrc", normed, bias_weight, preferred_element_type=jnp.float32
-    ).astype(jnp.bfloat16)
-    row_start = lax.axis_index("row") * rows_here
-    col_start = lax.axis_index("col") * width
-    residual = lax.dynamic_slice(single_rep, (row_start, col_start), (rows_here, width))
-    out_pieces = single_out_weight.reshape(width, cols, width).transpose(1, 0, 2)
+    single_proj_t = single_proj.transpose(0, 2, 1)
     bf16, f32 = jnp.bfloat16, jnp.float32
     dma = pltpu.SemaphoreType.DMA
     anywhere = pl.BlockSpec(memory_space=pl.ANY)
     held = pl.BlockSpec(memory_space=pltpu.VMEM)
     pair_out, single_out = pl.pallas_call(
         window_kernel,
-        in_specs=[pl.BlockSpec(memory_space=pltpu.SMEM), anywhere] + [held] * 11,
+        in_specs=[pl.BlockSpec(memory_space=pltpu.SMEM)] + [anywhere] * 6 + [held] * 5,
         out_specs=[anywhere, held],
         out_shape=[
             jax.ShapeDtypeStruct(pair_rep.shape, bf16),
             jax.ShapeDtypeStruct((rows_here, width), bf16),
         ],
         scratch_shapes=[
+            pltpu.VMEM(pair_rep.shape, bf16),
+            pltpu.VMEM((heads, rows_here, cols_here), f32),
+            pltpu.VMEM((heads, rows_here, cols_here), bf16),
+            pltpu.VMEM(single_rep.shape, bf16),
+            pltpu.VMEM(pair_proj.shape, bf16),
+            pltpu.VMEM(pair_out_weight.shape, bf16),
+            pltpu.VMEM(single_proj_t.shape, bf16),
+            pltpu.VMEM(single_out_weight.shape, bf16),
+            pltpu.VMEM((rows_here, width), bf16),
+            dma((cols,)),
+            dma((5,)),
             pltpu.VMEM((slab_rows, cols, cols_here, channels), bf16),
             pltpu.VMEM((slab_rows, cols, cols_here, channels), bf16),
             pltpu.VMEM((rows, cols, heads, rows_here, cols_here), bf16),
@@ -397,9 +466,8 @@
         ),
         name="window",
     )(
-        length, pair_rep, local_bias, single_rep, residual, pair_gain[None], pair_proj,
-        pair_out_weight, bias_norm_gain[None], single_bias_weight.T, single_gain[None],
-        single_proj, out_pieces,
+        length, pair_rep, single_rep, pair_proj, pair_out_weight, single_proj_t, single_out_weight,
+        pair_gain, bias_weight.T, bias_norm_gain, single_bias_weight.T, single_gain,
     )
     return (pair_out, single_out)
 

time: 147 us -> 132 us (0.90)
  local copies, waits for them, and re-layouts: 10.9 us -> 3.84 us
  other arithmetic: 4.23 us -> 0 us
  Pallas kernels: 128 us -> 126 us
  matrix products: 1.99 us -> 0 us
    reduce_sum x2 -> x0, other arithmetic: 4.22 us -> none  [the longest x1 2.56 us: normalize(): center = jnp.mean(floated, axis=-1, keepdims=True)]
    reshape x2 -> x0, local copies, waits for them, and re-layouts: 2.13 us -> none  [per_device(): single_out_weight.reshape(width, cols, width).transpose(1, 0, 2)]
    dot_general x1 -> x0, matrix products: 1.99 us -> none  [per_device(): jnp.einsum('rcd,dh->hrc', normed, bias_weight, preferred_element_type=jnp...]
    unnamed x13 -> x4, local copies, waits for them, and re-layouts: 5.4 us -> 3.84 us
where the time goes in v3:
time: 132 us; the launch traced here: 131 us
  Pallas kernels  126 us (95%)
  local copies, waits for them, and re-layouts  3.84 us (3%)
    pallas_call x1, Pallas kernels, per_device(): pl.pallas_call(window_kernel, in_specs=[pl.BlockSpec(memory_space=pltpu.S...  126 us
    unnamed x4, local copies, waits for them, and re-layouts  3.84 us

profile of v3, /device:TPU:0, one launch (start us, length us, event | category | flops | bytes accessed | tf_op | source)
XLA Modules:
  0.0 131.5 jit_solution(12787853646631802835)
XLA Ops:
  1.3 126.3 %window.1 = (bf16[48,96,256]{2,1,0:T(8,128)(2,1)}, bf16[48,192]{1,0:T(8,128)(2,1)}) custom-call(s32[1]{0:T(128)S(6)} %copy.16.length_ref, bf16[48,96,256]{2,1,0:T(8,128)(2,1)} %pair_ref.1, bf16[384,768]{1,0:T(8,128)(2,1)} %single_hbm.1, bf16[4,256,256]{2,1,0:T(8,128)(2,1)} %proj_hbm.1, bf16[256,256]{1,0:T(8,128)(2,1)} %out_weight_hbm.1, ...), custom_call_target="tpu_custom_call" | custom-call | tf_op jit(solution)/shard_map/window/pallas_call | solution.py:412
  127.6 0.0 copy-start
  127.6 3.2 %copy.17 = bf16[48,96,256]{2,1,0:T(8,128)(2,1)} copy(bf16[48,96,256]{2,1,0:T(8,128)(2,1)} %get-tuple-element.4) | data formatting | bytes 4718592
  130.8 0.0 copy-done
  130.9 0.6 copy.18
Async XLA Ops:
  127.6 3.2 %copy-start = (bf16[48,192]{1,0:T(8,128)(2,1)S(1)}, bf16[48,192]{1,0:T(8,128)(2,1)}, u32[]{:S(2)}) copy-start(bf16[48,192]{1,0:T(8,128)(2,1)} %get-tuple-element.5) | copy-start | bytes 55300

commit v4 on v3

--- a/solution.py
+++ b/solution.py
@@ -141,9 +141,20 @@
             device_id=to, device_id_type=mesh_id,
         )
 
+    near = cols // 2
+    mirror = peer(near)
+
+    def near_peer(step):
+        return col // near * near + lax.rem(lax.rem(col, near) + step, near)
+
+    own_steps = range(1, near)
+    mirror_steps = range(near + 1, 2 * near)
+
     def col_copy(step):
-        return remote(
-            tri_ref, slot(bands, row, col), col_send.at[step], col_recv.at[step], (row, peer(step))
+        to = mirror if step == 0 else near_peer(step % near)
+        src, place = (tri_ref, col) if step < near else (slot(bands, row, mirror), mirror)
+        return remote(
+            src, slot(bands, row, place), col_send.at[step], col_recv.at[step], (row, to)
         )
 
     def chip_copy(step):
@@ -217,19 +228,26 @@
                 )
 
     tri_ref[...] = tri_kept[...].astype(jnp.bfloat16)
-    for step in range(1, cols):
+    for step in (0, *own_steps):
         col_copy(step).start()
     own_block = pltpu.make_async_copy(tri_ref, slot(bands, row, col), col_own)
     own_block.start()
 
-    @pl.loop(1, slab_rows)
+    ahead = min(3, slab_rows)
+    for s in range(1, ahead):
+        bring_row(s)
+    col_copy(0).wait_recv()
+    for step in mirror_steps:
+        col_copy(step).start()
+
+    @pl.loop(ahead, slab_rows)
     def _(s):
         bring_row(s)
 
     for copy in weight_copies:
         copy.wait()
 
-    for step in range(1, cols):
+    for step in (*own_steps, *mirror_steps):
         col_copy(step).wait_recv()
     own_block.wait()
     for step in range(1, chips):
@@ -364,9 +382,10 @@
     single_new_ref[...] = total.astype(jnp.bfloat16)
 
     for step in range(1, cols):
-        col_copy(step).wait_send()
         head_copy(step).wait_send()
         part_copy(step).wait_send()
+    for step in (0, *own_steps, *mirror_steps):
+        col_copy(step).wait_send()
     for step in range(1, chips):
         chip_copy(step).wait_send()
     for step in range(chips):

time: 132 us -> 127 us (0.962)
  Pallas kernels: 126 us -> 122 us
    pallas_call x1, Pallas kernels: 126 us -> 122 us  [per_device(): pl.pallas_call(window_kernel, in_specs=[pl.BlockSpec(memory_space=pltpu.S...]
where the time goes in v4:
time: 127 us
  Pallas kernels  122 us (96%)
  local copies, waits for them, and re-layouts  3.84 us (3%)
  between operations  1.3 us (1%)
    pallas_call x1, Pallas kernels, per_device(): pl.pallas_call(window_kernel, in_specs=[pl.BlockSpec(memory_space=pltpu.S...  122 us
    unnamed x4, local copies, waits for them, and re-layouts  3.84 us

profile of v4, /device:TPU:0, one launch (start us, length us, event | category | flops | bytes accessed | tf_op | source)
XLA Modules:
  0.0 127.3 jit_solution(8531980896876777988)
XLA Ops:
  1.3 122.2 %window.1 = (bf16[48,96,256]{2,1,0:T(8,128)(2,1)}, bf16[48,192]{1,0:T(8,128)(2,1)}) custom-call(s32[1]{0:T(128)S(6)} %copy.16.length_ref, bf16[48,96,256]{2,1,0:T(8,128)(2,1)} %pair_ref.1, bf16[384,768]{1,0:T(8,128)(2,1)} %single_hbm.1, bf16[4,256,256]{2,1,0:T(8,128)(2,1)} %proj_hbm.1, bf16[256,256]{1,0:T(8,128)(2,1)} %out_weight_hbm.1, ...), custom_call_target="tpu_custom_call" | custom-call | tf_op jit(solution)/shard_map/window/pallas_call | solution.py:431
  123.4 0.0 copy-start
  123.5 3.2 %copy.17 = bf16[48,96,256]{2,1,0:T(8,128)(2,1)} copy(bf16[48,96,256]{2,1,0:T(8,128)(2,1)} %get-tuple-element.4) | data formatting | bytes 4718592
  126.7 0.0 copy-done
  126.7 0.6 copy.18
Async XLA Ops:
  123.4 3.2 %copy-start = (bf16[48,192]{1,0:T(8,128)(2,1)S(1)}, bf16[48,192]{1,0:T(8,128)(2,1)}, u32[]{:S(2)}) copy-start(bf16[48,192]{1,0:T(8,128)(2,1)} %get-tuple-element.5) | copy-start | bytes 55300
